TPU v7x, 256 devices: a whole 4x4x8 slice. The times are simulated.
256 devices in a mesh: dp: 32 (over x, z), expert: 8 (over y, core).
Axes of the slice: x: 4, y: 4, z: 8, core: 2. Of those that a mesh axis runs over, the one named last changes fastest.
Arguments:
- tokens: bfloat16 [4096, 4096], P('dp', 'expert'), may hold values from -6 to 6
- expert_ids: int32 [4096, 8], P('dp'), may hold values from 0 to 31, all different within a row; in each aligned block of 128 rows (0 to 127, 128 to 255, ...) at most 40 rows name the same one
- scores: float32 [4096, 8], P('dp'), may hold values from 0.05 to 1
- weight_in: bfloat16 [32, 4096, 2048], P('dp', 'expert'), may hold values from -0.09375 to 0.09375
- weight_out: bfloat16 [32, 1024, 4096], P('dp', None, 'expert'), may hold values from -0.1875 to 0.1875
- out_grad: bfloat16 [4096, 4096], P('dp', 'expert'), may hold values from -6 to 6
Outputs:
- layer_out: bfloat16 [4096, 4096], P('dp', 'expert')
- tokens_grad: bfloat16 [4096, 4096], P('dp', 'expert')
- scores_grad: float32 [4096, 8], P('dp')
- w_in_grad: bfloat16 [32, 4096, 2048], P('dp', 'expert')
- w_out_grad: bfloat16 [32, 1024, 4096], P('dp', None, 'expert')
Inputs may be any that keep to these rules, and one draw needn't show every extreme that they name: `expert_ids`: the 8 experts of a token differ. Among the 128 consecutive tokens of one index of dp no expert is named by more than 40 choices, and in every draw some such block names some expert exactly 40 times.
All inputs are finite; a program needn't handle non-finite values.
Results may differ from a plain program's by a relative error of at most 0.0064.
Values may be sent and summed in bfloat16 or wider, within the bound.
No kernel may reach another device: no remote copies, remote signals or barrier semaphores. Data moves between devices by JAX's collectives and lax.ppermute only.
A program may use at most 128 MiB of HBM per device.

v0:
```python
import jax
import jax.numpy as jnp
from jax import lax
from jax.sharding import PartitionSpec as P

ROUTE_SCALE = 2.5


def gate_terms(gate_up, hidden_units):
    gate = gate_up[:, :hidden_units]
    upward = gate_up[:, hidden_units:]
    return (gate, upward, jax.nn.sigmoid(gate))


def gate_backward(hidden_grad, gate, upward, sigma):
    return jnp.concatenate(
        [hidden_grad * upward * sigma * (1.0 + gate * (1.0 - sigma)), hidden_grad * gate * sigma],
        axis=1,
    ).astype(jnp.bfloat16)


def body(tokens, expert_ids, scores, weight_in, weight_out, out_grad):
    n_data = lax.axis_size("dp")
    tok_count, slab_width = tokens.shape
    top_count = expert_ids.shape[1]
    hidden_units = weight_out.shape[1]
    capacity = min(tok_count, 5 * tok_count * top_count // (4 * n_data))
    routed = tok_count * top_count
    group_rows = n_data * capacity
    slot_count = n_data * capacity
    flat_ids = expert_ids.reshape(routed)
    expert_hot = (flat_ids[:, None] == jnp.arange(n_data, dtype=jnp.int32)[None, :]).astype(
        jnp.int32
    )
    earlier = jnp.sum((jnp.cumsum(expert_hot, axis=0) - expert_hot) * expert_hot, axis=1)
    target = flat_ids * capacity + earlier
    placing = (jnp.arange(slot_count, dtype=jnp.int32)[:, None] == target[None, :]).astype(
        jnp.bfloat16
    )
    token_place = jnp.sum(
        placing.reshape(slot_count, tok_count, top_count).astype(jnp.float32), axis=2
    ).astype(jnp.bfloat16)
    score_total = jnp.sum(scores, axis=1, keepdims=True)
    route_weights = ROUTE_SCALE * scores / score_total
    routed_grad = (route_weights[:, :, None] * out_grad.astype(jnp.float32)[:, None, :]).astype(
        jnp.bfloat16
    )
    routed_grad = routed_grad.reshape(routed, slab_width)
    token_send = jnp.dot(token_place, tokens, preferred_element_type=jnp.float32).astype(
        jnp.bfloat16
    )
    grad_send = jnp.dot(placing, routed_grad, preferred_element_type=jnp.float32).astype(
        jnp.bfloat16
    )
    token_slab, grad_slab = (
        lax.all_to_all(
            token_send.reshape(n_data, capacity, slab_width),
            "dp",
            split_axis=0,
            concat_axis=0,
            tiled=True,
        ),
        lax.all_to_all(
            grad_send.reshape(n_data, capacity, slab_width),
            "dp",
            split_axis=0,
            concat_axis=0,
            tiled=True,
        ),
    )
    token_slab = token_slab.reshape(group_rows, slab_width)
    grad_slab = grad_slab.reshape(group_rows, slab_width)
    in_slab = weight_in[0]
    out_slab = weight_out[0]
    gate_up_own = lax.psum_scatter(
        jnp.dot(token_slab, in_slab, preferred_element_type=jnp.float32),
        "expert",
        scatter_dimension=0,
        tiled=True,
    )
    gate_own, up_own, sig_own = gate_terms(gate_up_own, hidden_units)
    hidden_own = (gate_own * sig_own * up_own).astype(jnp.bfloat16)
    piece = lax.all_gather(hidden_own, "expert", axis=0, tiled=True)
    product = jnp.dot(piece, out_slab, preferred_element_type=jnp.float32)
    out_rows = product
    weight_sum = jnp.einsum("rf,rd->fd", piece, grad_slab, preferred_element_type=jnp.float32)
    out_rows, out_weight_sum = (out_rows, weight_sum)
    expert_out = out_rows.astype(jnp.bfloat16)
    out_blocks = expert_out.reshape(n_data, capacity, slab_width)
    out_back = lax.all_to_all(out_blocks, "dp", split_axis=0, concat_axis=0, tiled=True)
    hidden_grad = lax.psum_scatter(
        jnp.einsum("rd,fd->rf", grad_slab, out_slab, preferred_element_type=jnp.float32),
        "expert",
        scatter_dimension=0,
        tiled=True,
    )
    gate_up_grad = gate_backward(hidden_grad, gate_own, up_own, sig_own)
    piece = lax.all_gather(gate_up_grad, "expert", axis=0, tiled=True)
    product = jnp.einsum("rh,dh->rd", piece, in_slab, preferred_element_type=jnp.float32)
    input_rows = product
    weight_sum = jnp.einsum("rd,rh->dh", token_slab, piece, preferred_element_type=jnp.float32)
    input_rows, in_weight_sum = (input_rows, weight_sum)
    grad_blocks = input_rows.astype(jnp.bfloat16).reshape(n_data, capacity, slab_width)
    grad_back = lax.all_to_all(grad_blocks, "dp", split_axis=0, concat_axis=0, tiled=True)
    outputs_in = out_back.reshape(slot_count, slab_width)
    grads_in = grad_back.reshape(slot_count, slab_width)
    picked = jnp.einsum("sr,sd->rd", placing, outputs_in, preferred_element_type=jnp.float32)
    picked = picked.reshape(tok_count, top_count, slab_width)
    layer_out = jnp.sum(route_weights[:, :, None] * picked, axis=1).astype(jnp.bfloat16)
    partial_dot = jnp.sum(out_grad.astype(jnp.float32)[:, None, :] * picked, axis=2)
    choice_dot = lax.psum(partial_dot, "expert")
    scores_grad = (
        ROUTE_SCALE * choice_dot - jnp.sum(choice_dot * route_weights, axis=1, keepdims=True)
    ) / score_total
    tokens_grad = jnp.einsum(
        "st,sd->td", token_place, grads_in, preferred_element_type=jnp.float32
    ).astype(jnp.bfloat16)
    return (
        layer_out,
        tokens_grad,
        scores_grad,
        in_weight_sum.astype(jnp.bfloat16)[None],
        out_weight_sum.astype(jnp.bfloat16)[None],
    )


def solution(mesh):
    placed = (
        P("dp", "expert"),
        P("dp", None),
        P("dp", None),
        P("dp", "expert", None),
        P("dp", None, "expert"),
        P("dp", "expert"),
    )
    return jax.shard_map(
        body,
        mesh=mesh,
        in_specs=placed,
        out_specs=(
            P("dp", "expert"),
            P("dp", "expert"),
            P("dp", None),
            P("dp", "expert", None),
            P("dp", None, "expert"),
        ),
        check_vma=False,
    )
```

profile of v0, /device:TPU:33, one launch (start us, length us, event | category | flops | bytes accessed | tf_op | source)
XLA Modules:
  0.0 320.6 jit_solution(14053334672853619055)
XLA Ops:
  7.2 0.0 copy-start
  7.2 0.0 reduce-scatter.5.cloned.1.call-start
  7.2 0.9 copy.31
  8.2 0.1 eq.62
  8.2 0.1 reshape.105
  8.4 9.0 %reduce-window.6 = s32[32,8,128]{2,1,0:T(8,128)S(1)} reduce-window(s32[32,8,128]{2,1,0:T(8,128)S(1)} %fusion.23, s32[]{:T(128)} %constant.13.clone.1), window={size=1x1x128 pad=0_0x0_0x127_0}, to_apply=%region_1.2 | reduce-window | flops 4161536 | bytes 262148 | tf_op jit(solution)/shard_map/reduce-window
  17.4 0.1 slice.16
  17.5 0.1 copy.33
  17.6 0.1 copy.34
  17.7 0.1 broadcast_add_fusion
  17.9 0.7 reduce_sum.59
  18.6 0.7 multiply_divide_fusion
  19.3 0.1 copy.37
  19.4 0.1 mul.93
  19.5 0.9 convert_element_type.56
  20.4 0.0 copy-start.6
  20.4 1.6 fusion.5
  22.0 0.0 copy-done.6
  22.0 0.0 copy-start.11
  22.1 44.8 %all_to_all.20 = bf16[32,40,512]{2,1,0:T(8,128)(2,1)S(1)} all-to-all(bf16[32,40,512]{2,1,0:T(8,128)(2,1)S(1)} %bitcast.71), channel_id=1, replica_groups=mesh['dp'=32,'expert'=8] {'dp'}, dimensions={0} | all-to-all | bytes 2621440 | tf_op jit(solution)/shard_map/all_to_all | solution.py:63
  66.8 1.1 copy-done.2
  67.9 0.0 copy-done.11
  67.9 3.9 %fusion.16 = f32[1280,1024]{1,0:T(8,128)} fusion(bf16[1280,512]{1,0:T(8,128)(2,1)S(1)} %bitcast.64, bf16[1,1024,512]{2,1,0:T(8,128)(2,1)S(1)} %copy-done.11), kind=kOutput, calls=%fused_computation.27 | convolution fusion | flops 1342177280 | bytes 7602176 | tf_op jit(solution)/shard_map/rd,fd->rf/dot_general | solution.py:92
  71.8 0.0 reduce-scatter.5.cloned.1.call-update
  71.9 0.0 reduce-scatter.3.cloned.1.call-start
  71.9 0.1 reduce_sum.61
  72.0 0.5 copy-done.10
  72.5 6.7 %fusion.7 = bf16[1280,128]{1,0:T(8,128)(2,1)S(1)} fusion(s32[128,8]{0,1:T(8,128)S(1)} %multiply_add_fusion), kind=kLoop, calls=%fused_computation.14 | loop fusion | flops 3768320 | bytes 331776 | tf_op jit(solution)/shard_map/reduce_sum | solution.py:40
  79.2 0.0 copy-done.8
  79.2 0.0 copy-start.1
  79.2 0.5 convolution_convert_fusion.3
  79.7 38.6 %all_to_all.21 = bf16[32,40,512]{2,1,0:T(8,128)(2,1)S(1)} all-to-all(bf16[32,40,512]{2,1,0:T(8,128)(2,1)S(1)} %bitcast.63), channel_id=1, replica_groups=mesh['dp'=32,'expert'=8] {'dp'}, dimensions={0} | all-to-all | bytes 2621440 | tf_op jit(solution)/shard_map/all_to_all | solution.py:56
  118.3 0.0 copy-done.1
  118.3 1.1 copy-done.3
  119.4 0.0 copy-done
  119.4 5.5 %fusion.11 = f32[1280,2048]{1,0:T(8,128)} fusion(bf16[1280,512]{1,0:T(8,128)(2,1)S(1)} %bitcast.66, bf16[1,512,2048]{2,1,0:T(8,128)(2,1)S(1)} %copy-done), kind=kOutput, calls=%fused_computation.19 | convolution fusion | flops 2684354560 | bytes 13893632 | tf_op jit(solution)/shard_map/dot_general | solution.py:76
  124.9 0.0 reduce-scatter.3.cloned.1.call-update
  124.9 0.0 all-gather.3.cloned.1.call-start
  125.0 0.0 reduce-scatter.5.cloned.1.call-done
  125.0 62.0 %reduce-scatter.3.cloned.1.call-done = f32[160,2048]{1,0:T(8,128)} async-done(((f32[1280,2048]{1,0:T(8,128)}), f32[160,2048]{1,0:T(8,128)}) %reduce-scatter.3.cloned.1.call-update) | async-done | bytes 1310736 | tf_op jit(solution)/shard_map/reduce_scatter | solution.py:75
  187.0 2.7 multiply_convert_fusion.1
  189.6 0.0 all-gather.3.cloned.1.call-update
  189.7 0.0 all-gather.5.cloned.1.call-start
  189.7 0.9 pad_maximum_fusion
  190.6 0.0 all-gather.5.cloned.1.call-update
  190.6 28.3 %all-gather.3.cloned.1.call-done = bf16[1280,1024]{1,0:T(8,128)(2,1)} async-done(((bf16[160,1024]{1,0:T(8,128)(2,1)}), bf16[1280,1024]{1,0:T(8,128)(2,1)}) %all-gather.3.cloned.1.call-update) | async-done | bytes 2621456 | tf_op jit(solution)/shard_map/all_gather | solution.py:83
  219.0 4.6 %convolution_convert_fusion.2 = bf16[1280,512]{1,0:T(8,128)(2,1)} fusion(bf16[1280,1024]{1,0:T(8,128)(2,1)} %all-gather.3.cloned.1.call-done, bf16[1,1024,512]{2,1,0:T(8,128)(2,1)} %param.10), kind=kOutput, calls=%fused_computation.11 | convolution fusion | flops 1342832640 | bytes 4980736 | tf_op jit(solution)/shard_map/dot_general | solution.py:84
  223.6 9.5 %all-to-all-start.1 = ((bf16[32,40,512]{2,1,0:T(8,128)(2,1)}), bf16[32,40,512]{2,1,0:T(8,128)(2,1)S(1)}, u32[]{:S(2)}, u32[]{:S(2)}) async-start(bf16[32,40,512]{2,1,0:T(8,128)(2,1)} %bitcast.70), calls=%async_computation.2 | async-start | bytes 2621440 | tf_op jit(solution)/shard_map/all_to_all | solution.py:90
  233.1 27.7 %all-gather.5.cloned.1.call-done = bf16[1280,2048]{1,0:T(8,128)(2,1)} async-done(((bf16[160,2048]{1,0:T(8,128)(2,1)}), bf16[1280,2048]{1,0:T(8,128)(2,1)}) %all-gather.5.cloned.1.call-update) | async-done | bytes 5242896 | tf_op jit(solution)/shard_map/all_gather | solution.py:98
  260.8 6.6 %convolution_convert_fusion.1 = bf16[1280,512]{1,0:T(8,128)(2,1)} fusion(bf16[1280,2048]{1,0:T(8,128)(2,1)} %all-gather.5.cloned.1.call-done, bf16[1,512,2048]{2,1,0:T(8,128)(2,1)S(1)} %copy-done), kind=kOutput, calls=%fused_computation.10 | convolution fusion | flops 2685009920 | bytes 8650752 | tf_op jit(solution)/shard_map/rh,dh->rd/dot_general | solution.py:99
  267.4 0.0 all-to-all-done.1
  267.4 1.1 copy-done.4
  268.5 9.5 %all-to-all-start.3 = ((bf16[32,40,512]{2,1,0:T(8,128)(2,1)}), bf16[32,40,512]{2,1,0:T(8,128)(2,1)S(1)}, u32[]{:S(2)}, u32[]{:S(2)}) async-start(bf16[32,40,512]{2,1,0:T(8,128)(2,1)} %bitcast.68), calls=%async_computation.5 | async-start | bytes 2621440 | tf_op jit(solution)/shard_map/all_to_all | solution.py:104
  277.9 0.8 fusion
  278.8 0.0 copy-start.5
  278.8 0.0 copy-start.7
  278.8 4.7 %fusion.13 = bf16[1,1024,512]{2,1,0:T(8,128)(2,1)} fusion(bf16[1280,1024]{1,0:T(8,128)(2,1)} %all-gather.3.cloned.1.call-done, bf16[1280,512]{1,0:T(8,128)(2,1)} %bitcast.65), kind=kOutput, calls=%fused_computation.24 | convolution fusion | flops 1342701568 | bytes 4980736 | tf_op jit(solution)/shard_map/rf,rd->fd/dot_general | solution.py:86
  283.5 0.0 copy-done.5
  283.5 2.3 multiply_reduce_fusion
  285.8 12.9 %psum.7 = f32[128,8]{0,1:T(8,128)S(1)} all-reduce(f32[128,8]{0,1:T(8,128)S(1)} %get-tuple-element.5), channel_id=1, replica_groups=mesh['dp'=32,'expert'=8] {'expert'}, use_global_device_ids=true, to_apply=%region_9.10 | all-reduce | flops 1024 | bytes 8192 | tf_op jit(solution)/shard_map/psum | solution.py:111
  298.7 0.6 subtract_divide_fusion
  299.3 7.1 %fusion.6 = bf16[1,512,2048]{2,1,0:T(8,128)(2,1)} fusion(bf16[1280,512]{1,0:T(8,128)(2,1)} %bitcast.67, bf16[1280,2048]{1,0:T(8,128)(2,1)} %all-gather.5.cloned.1.call-done), kind=kOutput, calls=%fused_computation.13 | convolution fusion | flops 2685403136 | bytes 8650752 | tf_op jit(solution)/shard_map/rd,rh->dh/dot_general | solution.py:101
  306.5 5.6 %all-to-all-done.3 = bf16[32,40,512]{2,1,0:T(8,128)(2,1)S(1)} async-done(((bf16[32,40,512]{2,1,0:T(8,128)(2,1)}), bf16[32,40,512]{2,1,0:T(8,128)(2,1)S(1)}, u32[]{:S(2)}, u32[]{:S(2)}) %all-to-all-start.3) | async-done | bytes 1310752 | tf_op jit(solution)/shard_map/all_to_all | solution.py:104
  312.0 2.0 convolution_convert_fusion.5
  (16 shorter events, 0.2 us)
Async XLA Ops:
  7.2 112.2 %copy-start = (bf16[1,512,2048]{2,1,0:T(8,128)(2,1)S(1)}, bf16[1,512,2048]{2,1,0:T(8,128)(2,1)}, u32[]{:S(2)}) copy-start(bf16[1,512,2048]{2,1,0:T(8,128)(2,1)} %param.9) | copy-start | bytes 6291460
  7.2 117.8 %reduce-scatter.5.cloned.1.call-start = ((), (), s32[]{:S(2)}) async-start(), calls=%async_computation.8 | async-start | bytes 5898240 | tf_op jit(solution)/shard_map/reduce_scatter | solution.py:91
  20.4 1.6 copy-start.6
  22.0 45.8 %copy-start.11 = (bf16[1,1024,512]{2,1,0:T(8,128)(2,1)S(1)}, bf16[1,1024,512]{2,1,0:T(8,128)(2,1)}, u32[]{:S(2)}) copy-start(bf16[1,1024,512]{2,1,0:T(8,128)(2,1)} %param.10) | copy-start | bytes 3145732
  66.8 1.1 copy-start.2
  71.8 0.7 copy-start.10
  71.8 7.4 %copy-start.8 = (bf16[128,512]{1,0:T(8,128)(2,1)S(1)}, bf16[128,512]{1,0:T(8,128)(2,1)}, u32[]{:S(2)}) copy-start(bf16[128,512]{1,0:T(8,128)(2,1)} %param.6) | copy-start | bytes 393220
  71.9 115.1 %reduce-scatter.3.cloned.1.call-start = ((), (), s32[]{:S(2)}) async-start(), calls=%async_computation.6 | async-start | bytes 11796480 | tf_op jit(solution)/shard_map/reduce_scatter | solution.py:75
  79.2 39.1 %copy-start.1 = (bf16[1280,128]{1,0:T(8,128)(2,1)}, bf16[1280,128]{1,0:T(8,128)(2,1)S(1)}, u32[]{:S(2)}) copy-start(bf16[1280,128]{1,0:T(8,128)(2,1)S(1)} %fusion.7) | copy-start | bytes 983044
  118.3 1.1 copy-start.3
  124.9 94.0 %all-gather.3.cloned.1.call-start = ((), (), s32[]{:S(2)}) async-start(), calls=%async_computation.7 | async-start | bytes 2949120 | tf_op jit(solution)/shard_map/all_gather | solution.py:83
  189.7 71.2 %all-gather.5.cloned.1.call-start = ((), (), s32[]{:S(2)}) async-start(), calls=%async_computation.9 | async-start | bytes 5898240 | tf_op jit(solution)/shard_map/all_gather | solution.py:98
  223.6 43.8 %all-to-all-start.1 = ((bf16[32,40,512]{2,1,0:T(8,128)(2,1)}), bf16[32,40,512]{2,1,0:T(8,128)(2,1)S(1)}, u32[]{:S(2)}, u32[]{:S(2)}) async-start(bf16[32,40,512]{2,1,0:T(8,128)(2,1)} %bitcast.70), calls=%async_computation.2 | async-start | bytes 2621440 | tf_op jit(solution)/shard_map/all_to_all | solution.py:90
  267.4 1.1 copy-start.4
  268.5 43.6 %all-to-all-start.3 = ((bf16[32,40,512]{2,1,0:T(8,128)(2,1)}), bf16[32,40,512]{2,1,0:T(8,128)(2,1)S(1)}, u32[]{:S(2)}, u32[]{:S(2)}) async-start(bf16[32,40,512]{2,1,0:T(8,128)(2,1)} %bitcast.68), calls=%async_computation.5 | async-start | bytes 2621440 | tf_op jit(solution)/shard_map/all_to_all | solution.py:104
  278.8 4.8 %copy-start.5 = (bf16[32,40,512]{2,1,0:T(8,128)(2,1)S(1)}, bf16[32,40,512]{2,1,0:T(8,128)(2,1)}, u32[]{:S(2)}) copy-start(bf16[32,40,512]{2,1,0:T(8,128)(2,1)} %copy-done.4) | copy-start | bytes 3932164
  278.8 4.8 %copy-start.7 = (f32[128,512]{1,0:T(8,128)S(1)}, f32[128,512]{1,0:T(8,128)}, u32[]{:S(2)}) copy-start(f32[128,512]{1,0:T(8,128)} %copy-done.6) | copy-start | bytes 786436
  283.5 15.2 %copy-start.9 = (f32[128,8]{0,1:T(8,128)S(1)}, f32[128,8]{0,1:T(8,128)}, u32[]{:S(2)}) copy-start(f32[128,8]{0,1:T(8,128)} %param.8) | copy-start | bytes 12292
Sparse Core Ops, SparseCore 0:
  72.0 37.5 reduce-scatter.4
  125.0 61.9 reduce-scatter.2
  189.8 29.1 all-gather.2
  221.2 39.5 all-gather.4
where the time goes:
time: 321 us
  waiting for transfers between devices  124 us (39%)
  blocking collectives  96.2 us (30%)
  matrix products  38.9 us (12%)
  other arithmetic  23.2 us (7%)
  starting transfers between devices  19.2 us (6%)
  between operations  14 us (4%)
  local copies, waits for them, and re-layouts  5.43 us (2%)
    reduce_scatter x1, waiting for transfers between devices, body(): lax.psum_scatter(jnp.dot(token_slab, in_slab, preferred_element_type=jnp....  62 us
    all_to_all x1, blocking collectives, body(): lax.all_to_all(grad_send.reshape(n_data, capacity, slab_width), 'dp', spl...  44.8 us
    all_to_all x1, blocking collectives, body(): lax.all_to_all(token_send.reshape(n_data, capacity, slab_width), 'dp', sp...  38.6 us
    all_gather x1, waiting for transfers between devices, body(): piece = lax.all_gather(hidden_own, 'expert', axis=0, tiled=True)  28.3 us
    all_gather x1, waiting for transfers between devices, body(): piece = lax.all_gather(gate_up_grad, 'expert', axis=0, tiled=True)  27.7 us
    psum x1, blocking collectives, body(): choice_dot = lax.psum(partial_dot, 'expert')  12.9 us
    another operation x4, other arithmetic  11.8 us
    all_to_all x1, starting transfers between devices, body(): lax.all_to_all(out_blocks, 'dp', split_axis=0, concat_axis=0, tiled=True)  9.53 us
  transfers between devices with their start and end apart: 6, of which 4 were waited for; matrix products, arithmetic and copies ran while one was open for 13% of the time, Pallas kernels for 0%

commit v1 on v0

--- a/solution.py
+++ b/solution.py
@@ -80,7 +80,10 @@
     )
     gate_own, up_own, sig_own = gate_terms(gate_up_own, hidden_units)
     hidden_own = (gate_own * sig_own * up_own).astype(jnp.bfloat16)
-    piece = lax.all_gather(hidden_own, "expert", axis=0, tiled=True)
+    peers = lax.axis_size("expert")
+    blocks = jnp.stack([hidden_own for _ in range(peers)])
+    blocks = lax.all_to_all(blocks, "expert", split_axis=0, concat_axis=0)
+    piece = jnp.concatenate(blocks, axis=0)
     product = jnp.dot(piece, out_slab, preferred_element_type=jnp.float32)
     out_rows = product
     weight_sum = jnp.einsum("rf,rd->fd", piece, grad_slab, preferred_element_type=jnp.float32)

time: 321 us -> 341 us (1.062)
  blocking collectives: 96.2 us -> 152 us
  waiting for transfers between devices: 124 us -> 89.1 us
    all_to_all x0 -> x1, blocking collectives: none -> 54.9 us  [body(): blocks = lax.all_to_all(blocks, 'expert', split_axis=0, concat_axis=0)]
    all_gather x1 -> x0, waiting for transfers between devices: 28.3 us -> none  [body(): piece = lax.all_gather(hidden_own, 'expert', axis=0, tiled=True)]
    all_gather x1, waiting for transfers between devices: 27.7 us -> 0.02 us  [body(): piece = lax.all_gather(gate_up_grad, 'expert', axis=0, tiled=True)]
    all_to_all x1, waiting for transfers between devices: 0.01 us -> 24.8 us  [body(): lax.all_to_all(out_blocks, 'dp', split_axis=0, concat_axis=0, tiled=True)]
  transfers between devices with their start and end apart: 6 -> 5, of which waited for: 4 -> 3; matrix products, arithmetic and copies ran while one was open for 13% -> 11% of each run, Pallas kernels for 0% -> 0%
where the time goes in v1:
time: 341 us; the launch traced here: 337 us
  blocking collectives  152 us (45%)
  waiting for transfers between devices  89.1 us (26%)
  matrix products  36.9 us (11%)
  other arithmetic  22.4 us (7%)
  starting transfers between devices  16.9 us (5%)
  between operations  14 us (4%)
  local copies, waits for them, and re-layouts  5.76 us (2%)
    reduce_scatter x1, waiting for transfers between devices, body(): lax.psum_scatter(jnp.dot(token_slab, in_slab, preferred_element_type=jnp....  62 us
    all_to_all x1, blocking collectives, body(): blocks = lax.all_to_all(blocks, 'expert', split_axis=0, concat_axis=0)  54.9 us
    all_to_all x1, blocking collectives, body(): lax.all_to_all(grad_send.reshape(n_data, capacity, slab_width), 'dp', spl...  44.8 us
    all_to_all x1, blocking collectives, body(): lax.all_to_all(token_send.reshape(n_data, capacity, slab_width), 'dp', sp...  38.6 us
    all_to_all x1, waiting for transfers between devices, body(): lax.all_to_all(out_blocks, 'dp', split_axis=0, concat_axis=0, tiled=True)  24.8 us
    psum x1, blocking collectives, body(): choice_dot = lax.psum(partial_dot, 'expert')  13.9 us
    another operation x4, other arithmetic  11.1 us
    all_to_all x1, starting transfers between devices, body(): lax.all_to_all(out_blocks, 'dp', split_axis=0, concat_axis=0, tiled=True)  9.5 us
  transfers between devices with their start and end apart: 5, of which 3 were waited for; matrix products, arithmetic and copies ran while one was open for 11% of the time, Pallas kernels for 0%

profile of v1, /device:TPU:33, one launch (start us, length us, event | category | flops | bytes accessed | tf_op | source)
XLA Modules:
  0.0 337.2 jit_solution(7834558228390054777)
XLA Ops:
  7.2 0.0 copy-start
  7.2 0.0 reduce-scatter.5.cloned.1.call-start
  7.2 0.9 copy.31
  8.2 0.1 eq.62
  8.2 0.1 reshape.110
  8.4 9.0 %reduce-window.6 = s32[32,8,128]{2,1,0:T(8,128)S(1)} reduce-window(s32[32,8,128]{2,1,0:T(8,128)S(1)} %fusion.23, s32[]{:T(128)} %constant.13.clone.1), window={size=1x1x128 pad=0_0x0_0x127_0}, to_apply=%region_1.2 | reduce-window | flops 4161536 | bytes 262148 | tf_op jit(solution)/shard_map/reduce-window
  17.4 0.1 slice.16
  17.5 0.1 copy.33
  17.6 0.1 copy.34
  17.7 0.1 broadcast_add_fusion
  17.9 0.7 reduce_sum.59
  18.6 0.7 multiply_divide_fusion
  19.3 0.1 copy.37
  19.4 0.1 mul.93
  19.5 0.9 convert_element_type.56
  20.4 0.0 copy-start.7
  20.4 1.6 fusion.5
  22.0 0.0 copy-done.7
  22.0 0.0 copy-start.12
  22.1 44.8 %all_to_all.25 = bf16[32,40,512]{2,1,0:T(8,128)(2,1)S(1)} all-to-all(bf16[32,40,512]{2,1,0:T(8,128)(2,1)S(1)} %bitcast.74), channel_id=1, replica_groups=mesh['dp'=32,'expert'=8] {'dp'}, dimensions={0} | all-to-all | bytes 2621440 | tf_op jit(solution)/shard_map/all_to_all | solution.py:63
  66.8 1.1 copy-done.3
  67.9 0.0 copy-done.12
  67.9 3.9 %fusion.16 = f32[1280,1024]{1,0:T(8,128)} fusion(bf16[1280,512]{1,0:T(8,128)(2,1)S(1)} %bitcast.67, bf16[1,1024,512]{2,1,0:T(8,128)(2,1)S(1)} %copy-done.12), kind=kOutput, calls=%fused_computation.27 | convolution fusion | flops 1342177280 | bytes 7602176 | tf_op jit(solution)/shard_map/rd,fd->rf/dot_general | solution.py:95
  71.8 0.0 reduce-scatter.5.cloned.1.call-update
  71.8 0.0 reduce-scatter.3.cloned.1.call-start
  71.9 0.1 reduce_sum.61
  72.0 0.5 copy-done.11
  72.5 6.7 %fusion.7 = bf16[1280,128]{1,0:T(8,128)(2,1)S(1)} fusion(s32[128,8]{0,1:T(8,128)S(1)} %multiply_add_fusion), kind=kLoop, calls=%fused_computation.14 | loop fusion | flops 3768320 | bytes 331776 | tf_op jit(solution)/shard_map/reduce_sum | solution.py:40
  79.2 0.0 copy-done.9
  79.2 0.0 copy-start.1
  79.2 0.5 convolution_convert_fusion.3
  79.7 38.6 %all_to_all.26 = bf16[32,40,512]{2,1,0:T(8,128)(2,1)S(1)} all-to-all(bf16[32,40,512]{2,1,0:T(8,128)(2,1)S(1)} %bitcast.64), channel_id=1, replica_groups=mesh['dp'=32,'expert'=8] {'dp'}, dimensions={0} | all-to-all | bytes 2621440 | tf_op jit(solution)/shard_map/all_to_all | solution.py:56
  118.3 0.0 copy-done.1
  118.3 1.1 copy-done.4
  119.4 0.0 copy-done
  119.4 5.5 %fusion.11 = f32[1280,2048]{1,0:T(8,128)} fusion(bf16[1280,512]{1,0:T(8,128)(2,1)S(1)} %bitcast.69, bf16[1,512,2048]{2,1,0:T(8,128)(2,1)S(1)} %copy-done), kind=kOutput, calls=%fused_computation.19 | convolution fusion | flops 2684354560 | bytes 13893632 | tf_op jit(solution)/shard_map/dot_general | solution.py:76
  124.9 0.0 reduce-scatter.3.cloned.1.call-update
  124.9 0.0 all-gather.2.cloned.1.call-start
  125.0 0.0 reduce-scatter.5.cloned.1.call-done
  125.0 62.0 %reduce-scatter.3.cloned.1.call-done = f32[160,2048]{1,0:T(8,128)} async-done(((f32[1280,2048]{1,0:T(8,128)}), f32[160,2048]{1,0:T(8,128)}) %reduce-scatter.3.cloned.1.call-update) | async-done | bytes 1310736 | tf_op jit(solution)/shard_map/reduce_scatter | solution.py:75
  187.0 1.9 multiply_convert_fusion.1
  188.9 0.9 pad_maximum_fusion
  189.8 0.0 all-gather.2.cloned.1.call-update
  189.8 0.3 stack.2
  190.2 0.0 copy-start.13
  190.2 54.9 %all_to_all.27 = bf16[8,160,1024]{2,1,0:T(8,128)(2,1)S(1)} all-to-all(bf16[8,160,1024]{2,1,0:T(8,128)(2,1)S(1)} %stack.2), channel_id=1, replica_groups=mesh['dp'=32,'expert'=8] {'expert'}, dimensions={0} | all-to-all | bytes 5242880 | tf_op jit(solution)/shard_map/all_to_all | solution.py:85
  245.1 2.6 convolution_convert_fusion.2
  247.7 9.5 %all-to-all-start.2 = ((bf16[32,40,512]{2,1,0:T(8,128)(2,1)}), bf16[32,40,512]{2,1,0:T(8,128)(2,1)S(1)}, u32[]{:S(2)}, u32[]{:S(2)}) async-start(bf16[32,40,512]{2,1,0:T(8,128)(2,1)} %bitcast.73), calls=%async_computation.3 | async-start | bytes 2621440 | tf_op jit(solution)/shard_map/all_to_all | solution.py:93
  257.2 0.0 all-gather.2.cloned.1.call-done
  257.2 6.6 %convolution_convert_fusion.1 = bf16[1280,512]{1,0:T(8,128)(2,1)} fusion(bf16[1280,2048]{1,0:T(8,128)(2,1)} %all-gather.2.cloned.1.call-done, bf16[1,512,2048]{2,1,0:T(8,128)(2,1)S(1)} %copy-done), kind=kOutput, calls=%fused_computation.10 | convolution fusion | flops 2685009920 | bytes 8650752 | tf_op jit(solution)/shard_map/rh,dh->rd/dot_general | solution.py:102
  263.8 24.8 %all-to-all-done.2 = bf16[32,40,512]{2,1,0:T(8,128)(2,1)S(1)} async-done(((bf16[32,40,512]{2,1,0:T(8,128)(2,1)}), bf16[32,40,512]{2,1,0:T(8,128)(2,1)S(1)}, u32[]{:S(2)}, u32[]{:S(2)}) %all-to-all-start.2) | async-done | bytes 1310752 | tf_op jit(solution)/shard_map/all_to_all | solution.py:93
  288.5 1.1 copy-done.5
  289.6 7.3 %all-to-all-start.4 = ((bf16[32,40,512]{2,1,0:T(8,128)(2,1)}), bf16[32,40,512]{2,1,0:T(8,128)(2,1)S(1)}, u32[]{:S(2)}, u32[]{:S(2)}) async-start(bf16[32,40,512]{2,1,0:T(8,128)(2,1)} %bitcast.71), calls=%async_computation.6 | async-start | bytes 2621440 | tf_op jit(solution)/shard_map/all_to_all | solution.py:107
  296.9 0.8 fusion
  297.7 0.0 copy-start.6
  297.7 0.0 copy-start.8
  297.7 4.7 %fusion.13 = bf16[1,1024,512]{2,1,0:T(8,128)(2,1)} fusion(bf16[1280,1024]{1,0:T(8,128)(2,1)} %bitcast.66, bf16[1280,512]{1,0:T(8,128)(2,1)} %bitcast.68), kind=kOutput, calls=%fused_computation.24 | convolution fusion | flops 1342701568 | bytes 4980736 | tf_op jit(solution)/shard_map/rf,rd->fd/dot_general | solution.py:89
  302.5 0.0 copy-done.8
  302.5 2.3 multiply_reduce_fusion
  304.8 13.9 %psum.7 = f32[128,8]{0,1:T(8,128)S(1)} all-reduce(f32[128,8]{0,1:T(8,128)S(1)} %get-tuple-element.5), channel_id=1, replica_groups=mesh['dp'=32,'expert'=8] {'expert'}, use_global_device_ids=true, to_apply=%region_9.10 | all-reduce | flops 1024 | bytes 8192 | tf_op jit(solution)/shard_map/psum | solution.py:114
  318.7 0.6 subtract_divide_fusion
  319.3 7.1 %fusion.6 = bf16[1,512,2048]{2,1,0:T(8,128)(2,1)} fusion(bf16[1280,512]{1,0:T(8,128)(2,1)} %bitcast.70, bf16[1280,2048]{1,0:T(8,128)(2,1)} %all-gather.2.cloned.1.call-done), kind=kOutput, calls=%fused_computation.13 | convolution fusion | flops 2685403136 | bytes 8650752 | tf_op jit(solution)/shard_map/rd,rh->dh/dot_general | solution.py:104
  326.5 2.2 all-to-all-done.4
  328.7 2.0 convolution_convert_fusion.5
  (19 shorter events, 0.2 us)
Async XLA Ops:
  7.2 112.2 %copy-start = (bf16[1,512,2048]{2,1,0:T(8,128)(2,1)S(1)}, bf16[1,512,2048]{2,1,0:T(8,128)(2,1)}, u32[]{:S(2)}) copy-start(bf16[1,512,2048]{2,1,0:T(8,128)(2,1)} %param.9) | copy-start | bytes 6291460
  7.2 117.8 %reduce-scatter.5.cloned.1.call-start = ((), (), s32[]{:S(2)}) async-start(), calls=%async_computation.8 | async-start | bytes 5898240 | tf_op jit(solution)/shard_map/reduce_scatter | solution.py:94
  20.4 1.6 copy-start.7
  22.0 45.8 %copy-start.12 = (bf16[1,1024,512]{2,1,0:T(8,128)(2,1)S(1)}, bf16[1,1024,512]{2,1,0:T(8,128)(2,1)}, u32[]{:S(2)}) copy-start(bf16[1,1024,512]{2,1,0:T(8,128)(2,1)} %param.10) | copy-start | bytes 3145732
  66.8 1.1 copy-start.3
  71.8 0.7 copy-start.11
  71.8 7.4 %copy-start.9 = (bf16[128,512]{1,0:T(8,128)(2,1)S(1)}, bf16[128,512]{1,0:T(8,128)(2,1)}, u32[]{:S(2)}) copy-start(bf16[128,512]{1,0:T(8,128)(2,1)} %param.6) | copy-start | bytes 393220
  71.8 115.1 %reduce-scatter.3.cloned.1.call-start = ((), (), s32[]{:S(2)}) async-start(), calls=%async_computation.7 | async-start | bytes 11796480 | tf_op jit(solution)/shard_map/reduce_scatter | solution.py:75
  79.2 39.1 %copy-start.1 = (bf16[1280,128]{1,0:T(8,128)(2,1)}, bf16[1280,128]{1,0:T(8,128)(2,1)S(1)}, u32[]{:S(2)}) copy-start(bf16[1280,128]{1,0:T(8,128)(2,1)S(1)} %fusion.7) | copy-start | bytes 983044
  118.3 1.1 copy-start.4
  124.9 132.3 %all-gather.2.cloned.1.call-start = ((), (), s32[]{:S(2)}) async-start(), calls=%async_computation.9 | async-start | bytes 5898240 | tf_op jit(solution)/shard_map/all_gather | solution.py:101
  190.2 54.9 %copy-start.13 = (bf16[1,1024,512]{2,1,0:T(8,128)(2,1)S(1)}, bf16[1,1024,512]{2,1,0:T(8,128)(2,1)}, u32[]{:S(2)}) copy-start(bf16[1,1024,512]{2,1,0:T(8,128)(2,1)} %param.10) | copy-start | bytes 3145732
  245.1 2.6 copy-start.2
  247.7 40.9 %all-to-all-start.2 = ((bf16[32,40,512]{2,1,0:T(8,128)(2,1)}), bf16[32,40,512]{2,1,0:T(8,128)(2,1)S(1)}, u32[]{:S(2)}, u32[]{:S(2)}) async-start(bf16[32,40,512]{2,1,0:T(8,128)(2,1)} %bitcast.73), calls=%async_computation.3 | async-start | bytes 2621440 | tf_op jit(solution)/shard_map/all_to_all | solution.py:93
  288.5 1.1 copy-start.5
  289.6 39.1 %all-to-all-start.4 = ((bf16[32,40,512]{2,1,0:T(8,128)(2,1)}), bf16[32,40,512]{2,1,0:T(8,128)(2,1)S(1)}, u32[]{:S(2)}, u32[]{:S(2)}) async-start(bf16[32,40,512]{2,1,0:T(8,128)(2,1)} %bitcast.71), calls=%async_computation.6 | async-start | bytes 2621440 | tf_op jit(solution)/shard_map/all_to_all | solution.py:107
  297.7 4.8 %copy-start.6 = (bf16[32,40,512]{2,1,0:T(8,128)(2,1)S(1)}, bf16[32,40,512]{2,1,0:T(8,128)(2,1)}, u32[]{:S(2)}) copy-start(bf16[32,40,512]{2,1,0:T(8,128)(2,1)} %copy-done.5) | copy-start | bytes 3932164
  297.7 4.8 %copy-start.8 = (f32[128,512]{1,0:T(8,128)S(1)}, f32[128,512]{1,0:T(8,128)}, u32[]{:S(2)}) copy-start(f32[128,512]{1,0:T(8,128)} %copy-done.7) | copy-start | bytes 786436
  302.5 16.2 %copy-start.10 = (f32[128,8]{0,1:T(8,128)S(1)}, f32[128,8]{0,1:T(8,128)}, u32[]{:S(2)}) copy-start(f32[128,8]{0,1:T(8,128)} %param.8) | copy-start | bytes 12292
Sparse Core Ops, SparseCore 0:
  72.0 37.5 reduce-scatter.4
  125.0 61.9 reduce-scatter.2
  189.9 58.9 all-gather.1
